TPU v7x, 32 devices: a whole 2x2x4 slice. The times are simulated.
32 devices in a mesh: shard: 8 (over y, x, core), rep: 4 (over z).
Axes of the slice: x: 2, y: 2, z: 4, core: 2. Of those that a mesh axis runs over, the one named last changes fastest.
Arguments:
- inputs: bfloat16 [64, 256, 1024], P(('shard', 'rep')), may hold values from -6 to 6
- lengths: int32 [64], replicated, may hold values from 64 to 256, as said below
- dealing: int32 [64], replicated, may hold values from 0 to 63, as said below
- w_query: bfloat16 [1024, 1024], P('shard'), may hold values from -0.25 to 0.25
- w_key: bfloat16 [1024, 1024], P('shard'), may hold values from -0.25 to 0.25
- w_value: bfloat16 [1024, 1024], P('shard'), may hold values from -0.1875 to 0.1875
- w_out: bfloat16 [1024, 1024], P('shard'), may hold values from -0.5 to 0.5
- b_query: bfloat16 [1024], P('shard'), may hold values from -1.5 to 1.5
- b_value: bfloat16 [1024], P('shard'), may hold values from -1.5 to 1.5
- b_out: bfloat16 [1024], P('shard'), may hold values from -1.5 to 1.5
- ln1_gain: bfloat16 [1024], P('shard'), may hold values from 0.099609375 to 1.8984375
- ln1_bias: bfloat16 [1024], P('shard'), may hold values from -1.5 to 1.5
- w_up: bfloat16 [1024, 4096], P('shard'), may hold values from -0.1875 to 0.1875
- b_up: bfloat16 [4096], P('shard'), may hold values from -1.5 to 1.5
- w_down: bfloat16 [4096, 1024], P('shard'), may hold values from -0.09375 to 0.09375
- b_down: bfloat16 [1024], P('shard'), may hold values from -1.5 to 1.5
- ln2_gain: bfloat16 [1024], P('shard'), may hold values from 0.099609375 to 1.8984375
- ln2_bias: bfloat16 [1024], P('shard'), may hold values from -1.5 to 1.5
- cotangent: bfloat16 [64, 256, 1024], P(('shard', 'rep')), may hold values from -6 to 6
Outputs:
- layer_out: bfloat16 [64, 256, 1024], P(('shard', 'rep'))
- grad_input: bfloat16 [64, 256, 1024], P(('shard', 'rep'))
- grad_w_query: float32 [1024, 1024], P('shard')
- grad_w_key: float32 [1024, 1024], P('shard')
- grad_w_value: float32 [1024, 1024], P('shard')
- grad_w_out: float32 [1024, 1024], P('shard')
- grad_b_query: float32 [1024], P('shard')
- grad_b_value: float32 [1024], P('shard')
- grad_b_out: float32 [1024], P('shard')
- grad_ln1_gain: float32 [1024], P('shard')
- grad_ln1_bias: float32 [1024], P('shard')
- grad_w_up: float32 [1024, 4096], P('shard')
- grad_b_up: float32 [4096], P('shard')
- grad_w_down: float32 [4096, 1024], P('shard')
- grad_b_down: float32 [1024], P('shard')
- grad_ln2_gain: float32 [1024], P('shard')
- grad_ln2_bias: float32 [1024], P('shard')
Inputs may be any that keep to these rules, and one draw needn't show every extreme that they name: `lengths`: length of initial sequence; positions at or past it are padding. `dealing`: a permutation of the 64 sequences that maps each aligned block of 8 positions onto itself.
All inputs are finite; a program needn't handle non-finite values.
Results may differ from a plain program's by a relative error of at most 0.02.
Values may be sent and summed in bfloat16 or wider, within the bound.
No kernel may reach another device: no remote copies, remote signals or barrier semaphores. Data moves between devices by JAX's collectives and lax.ppermute only.
A program may use at most 192 MiB of HBM per device.

v0:
```python
import jax
import jax.numpy as jnp
from jax import lax
from jax.sharding import PartitionSpec as P

H = 16
HD = 64
EPS = 1e-05
NEG = -1e30
F32 = jnp.float32
BF16 = jnp.bfloat16


def matmul(left, right):
    return jnp.dot(left, right, preferred_element_type=F32)


def left_trans(left, right):
    return lax.dot_general(left, right, (((0,), (0,)), ((), ())), preferred_element_type=F32)


def right_trans(left, right):
    return lax.dot_general(left, right, (((1,), (1,)), ((), ())), preferred_element_type=F32)


def normalize(values, gain, shift):
    center = values - jnp.mean(values, -1, keepdims=True)
    inverse = lax.rsqrt(jnp.mean(center * center, -1, keepdims=True) + EPS)
    unit = center * inverse
    return (unit * gain + shift, unit, inverse)


def norm_back(grad, unit, inverse, gain):
    scaled = grad * gain
    return inverse * (
        scaled
        - jnp.mean(scaled, -1, keepdims=True)
        - unit * jnp.mean(scaled * unit, -1, keepdims=True)
    )


def gelu_both(pre):
    cumul = 0.5 * (1.0 + lax.erf(pre * 0.7071067811865476))
    density = jnp.exp(-0.5 * pre * pre) * 0.3989422804014327
    return (pre * cumul, cumul + pre * density)


def pick(pool, targets):
    return jnp.stack(
        [
            lax.dynamic_index_in_dim(pool, targets[i], 0, keepdims=False)
            for i in range(targets.shape[0])
        ]
    )


def local(
    inputs,
    lengths,
    dealing,
    w_query,
    w_key,
    w_value,
    w_out,
    b_query,
    b_value,
    b_out,
    ln1_gain,
    ln1_bias,
    w_up,
    b_up,
    w_down,
    b_down,
    ln2_gain,
    ln2_bias,
    cotangent,
):
    batches, rows, width = inputs.shape
    shards = lax.axis_size("shard")
    replicas = lax.axis_size("rep")
    group = batches * replicas
    shard_index = lax.axis_index("shard")
    rep_index = lax.axis_index("rep")
    anchor = shard_index * group
    slots = anchor + rep_index * batches + jnp.arange(batches, dtype=jnp.int32)
    seq_lengths = jnp.take(lengths, slots)
    local_dealing = lax.dynamic_slice_in_dim(dealing, anchor, group) - anchor
    sources = jnp.take(dealing, slots) - anchor
    places = jnp.arange(group, dtype=jnp.int32)
    wanted = jnp.sum(
        jnp.where(local_dealing[None, :] == (slots - anchor)[:, None], places[None, :], 0), 1
    )

    def gather(block):
        return lax.all_gather(block, "shard", axis=0, tiled=True)

    block = w_query.shape[0]
    wide = w_up.shape[1]
    small = (b_query, b_value, b_out, ln1_gain, ln1_bias, b_down, ln2_gain, ln2_bias, b_up)
    vec = jnp.concatenate(small)
    first = jnp.concatenate([w_query, w_key, w_value, w_out], 0)
    all_vec = lax.all_gather(vec, "shard", axis=0, tiled=True).reshape(shards, -1)
    all_first = gather(first).reshape(shards, 4, block, width)
    cuts = [0]
    for part in small:
        cuts.append(cuts[-1] + part.shape[0])
    (
        bias_query,
        bias_value,
        bias_out,
        gain_one,
        shift_one,
        bias_down,
        gain_two,
        shift_two,
        bias_up,
    ) = [all_vec[:, cuts[i] : cuts[i + 1]].reshape(-1).astype(F32) for i in range(len(small))]
    full_query, full_key, full_value, full_out = [
        all_first[:, i].reshape(width, width) for i in range(4)
    ]
    full_up = gather(w_up)
    full_down = gather(w_down)
    cot = pick(lax.all_gather(cotangent, "rep", axis=0, tiled=True), wanted)
    tokens = inputs.reshape(batches * rows, width)
    query = (matmul(tokens, full_query) + bias_query).astype(BF16)
    keyed = matmul(tokens, full_key).astype(BF16)
    value = (matmul(tokens, full_value) + bias_value).astype(BF16)
    heads = lambda a: a.reshape(batches, rows, H, HD).transpose(0, 2, 1, 3)
    flat = lambda a: a.transpose(0, 2, 1, 3).reshape(batches * rows, width)
    qh, kh, vh = (heads(query), heads(keyed), heads(value))
    allowed = (
        lax.broadcasted_iota(jnp.int32, (batches, 1, 1, rows), 3) < seq_lengths[:, None, None, None]
    )
    scale = HD ** (-0.5)
    scores = jnp.einsum("bhqd,bhkd->bhqk", qh, kh, preferred_element_type=F32) * scale
    scores = jnp.where(allowed, scores, NEG)
    raised = jnp.exp(scores - jnp.max(scores, -1, keepdims=True))
    probs = raised / jnp.sum(raised, -1, keepdims=True)
    probs_low = probs.astype(BF16)
    mixed_low = flat(
        jnp.einsum("bhqk,bhkd->bhqd", probs_low, vh, preferred_element_type=F32).astype(BF16)
    )
    hidden, unit_one, inverse_one = normalize(
        tokens.astype(F32) + matmul(mixed_low, full_out) + bias_out, gain_one, shift_one
    )
    hidden_low = hidden.astype(BF16)
    pre = matmul(hidden_low, full_up) + bias_up
    act, slope = gelu_both(pre)
    act_low = act.astype(BF16)
    summed = hidden + matmul(act_low, full_down) + bias_down
    normed, unit_two, inverse_two = normalize(summed, gain_two, shift_two)
    valid = (
        lax.broadcasted_iota(jnp.int32, (batches, rows, 1), 1) < seq_lengths[:, None, None]
    ).reshape(-1, 1)
    out = jnp.where(valid, normed, 0.0).astype(BF16).reshape(batches, rows, width)
    layer_out = pick(lax.all_gather(out, "rep", axis=0, tiled=True), sources)
    grad_out = jnp.where(valid, cot.reshape(-1, width).astype(F32), 0.0)
    grad_gain_two = jnp.sum(grad_out * unit_two, 0)
    grad_shift_two = jnp.sum(grad_out, 0)
    grad_sum = norm_back(grad_out, unit_two, inverse_two, gain_two)
    grad_bias_down = jnp.sum(grad_sum, 0)
    grad_sum_low = grad_sum.astype(BF16)

    def reduced(part):
        return lax.psum_scatter(part, "shard", scatter_dimension=0, tiled=True)

    def over_rep(part):
        return lax.psum(part, "rep").astype(F32)

    g_down = reduced(left_trans(act_low, grad_sum_low).astype(BF16))
    grad_pre = (right_trans(grad_sum_low, full_down) * slope).astype(BF16)
    grad_bias_up = jnp.sum(grad_pre.astype(F32), 0)
    g_up = reduced(left_trans(hidden_low, grad_pre).astype(BF16))
    grad_hidden = grad_sum + right_trans(grad_pre, full_up)
    grad_gain_one = jnp.sum(grad_hidden * unit_one, 0)
    grad_shift_one = jnp.sum(grad_hidden, 0)
    grad_resid = norm_back(grad_hidden, unit_one, inverse_one, gain_one)
    grad_bias_out = jnp.sum(grad_resid, 0)
    grad_resid_low = grad_resid.astype(BF16)
    grad_w_out = left_trans(mixed_low, grad_resid_low).astype(BF16)
    grad_mixed = heads(right_trans(grad_resid_low, full_out).astype(BF16))
    grad_probs = jnp.einsum("bhqd,bhkd->bhqk", grad_mixed, vh, preferred_element_type=F32)
    inner = jnp.sum(probs * grad_probs, -1, keepdims=True)
    grad_scores = (probs * (grad_probs - inner) * scale).astype(BF16)
    query_low = flat(
        jnp.einsum("bhqk,bhkd->bhqd", grad_scores, kh, preferred_element_type=F32).astype(BF16)
    )
    key_low = flat(
        jnp.einsum("bhqk,bhqd->bhkd", grad_scores, qh, preferred_element_type=F32).astype(BF16)
    )
    value_low = flat(
        jnp.einsum("bhqk,bhqd->bhkd", probs_low, grad_mixed, preferred_element_type=F32).astype(
            BF16
        )
    )
    grad_bias_query = jnp.sum(query_low.astype(F32), 0)
    grad_bias_value = jnp.sum(value_low.astype(F32), 0)
    blocks = [
        part.reshape(shards, block, width)
        for part in (
            left_trans(tokens, query_low).astype(BF16),
            left_trans(tokens, key_low).astype(BF16),
            left_trans(tokens, value_low).astype(BF16),
            grad_w_out,
        )
    ]
    g_first = reduced(jnp.concatenate(blocks, 1).reshape(shards * 4 * block, width))
    grad_tokens = (
        grad_resid
        + right_trans(query_low, full_query)
        + right_trans(key_low, full_key)
        + right_trans(value_low, full_value)
    )
    grad_input = grad_tokens.astype(BF16).reshape(batches, rows, width)
    vec_terms = (
        grad_bias_query,
        grad_bias_value,
        grad_bias_out,
        grad_gain_one,
        grad_shift_one,
        grad_bias_down,
        grad_gain_two,
        grad_shift_two,
        grad_bias_up,
    )
    g_vec = jnp.concatenate([part.reshape(shards, -1) for part in vec_terms], 1)
    g_vec = lax.psum(g_vec, ("shard", "rep"))
    g_vec = lax.dynamic_index_in_dim(g_vec, shard_index, 0, keepdims=False)
    g_bquery, g_bvalue, g_bout, g_gain_one, g_shift_one, g_bdown, g_gain_two, g_shift_two, g_bup = [
        g_vec[cuts[i] : cuts[i + 1]] for i in range(len(small))
    ]
    g_down = over_rep(g_down)
    g_up = over_rep(g_up)
    g_first = over_rep(g_first).reshape(4, block, width)
    return (
        layer_out,
        grad_input,
        g_first[0],
        g_first[1],
        g_first[2],
        g_first[3],
        g_bquery,
        g_bvalue,
        g_bout,
        g_gain_one,
        g_shift_one,
        g_up,
        g_bup,
        g_down,
        g_bdown,
        g_gain_two,
        g_shift_two,
    )


def solution(mesh):
    seqs = P(("shard", "rep"), None, None)
    mat = P("shard", None)
    vec = P("shard")
    in_specs = (
        seqs,
        P(),
        P(),
        mat,
        mat,
        mat,
        mat,
        vec,
        vec,
        vec,
        vec,
        vec,
        mat,
        vec,
        mat,
        vec,
        vec,
        vec,
        seqs,
    )
    out_specs = (
        seqs,
        seqs,
        mat,
        mat,
        mat,
        mat,
        vec,
        vec,
        vec,
        vec,
        vec,
        mat,
        vec,
        mat,
        vec,
        vec,
        vec,
    )
    return jax.shard_map(local, mesh=mesh, in_specs=in_specs, out_specs=out_specs, check_vma=False)
```

profile of v0, /device:TPU:0, one launch (start us, length us, event | category | flops | bytes accessed | tf_op | source)
XLA Modules:
  0.0 790.4 jit_solution(13564791712874749416)
XLA Ops:
  18.1 10.6 %all-gather = bf16[8,1,1536]{2,1,0:T(2,128)(2,1)S(1)} all-gather(bf16[1,1,1536]{2,1,0:T(2,128)(2,1)S(1)} %reshape.383), channel_id=1, replica_groups=mesh['shard'=8,'rep'=4] {'shard'}, dimensions={0}, use_global_device_ids=true | all-gather | bytes 27648 | tf_op jit(solution)/shard_map/all_gather | solution.py:102
  30.9 62.3 %all-gather.15.cloned.1.call-done = bf16[8,256,1024]{2,1,0:T(8,128)(2,1)} async-done(((bf16[2,256,1024]{2,1,0:T(8,128)(2,1)}), bf16[8,256,1024]{2,1,0:T(8,128)(2,1)}) %all-gather.15.cloned.1.call-update) | async-done | bytes 4194320 | tf_op jit(solution)/shard_map/all_gather | solution.py:123
  95.5 53.0 %all-gather.7.cloned.1.call-done = bf16[4096,1024]{1,0:T(8,128)(2,1)} async-done(((bf16[512,1024]{1,0:T(8,128)(2,1)}), bf16[4096,1024]{1,0:T(8,128)(2,1)}) %all-gather.7.cloned.1.call-update) | async-done | bytes 8388624 | tf_op jit(solution)/shard_map/all_gather | solution.py:95
  148.5 5.9 fusion.97
  157.4 4.7 fusion.43
  163.5 4.5 fusion.53
  183.9 20.9 %all-gather.9.cloned.1.call-done = bf16[1024,4096]{1,0:T(8,128)(2,1)} async-done(((bf16[128,4096]{1,0:T(8,128)(2,1)}), bf16[1024,4096]{1,0:T(8,128)(2,1)}) %all-gather.9.cloned.1.call-update) | async-done | bytes 8388624 | tf_op jit(solution)/shard_map/all_gather | solution.py:95
  204.8 10.9 %multiply_convert_fusion.1 = (bf16[512,4096]{1,0:T(8,128)(2,1)}, f32[512,4096]{1,0:T(8,128)}) fusion(f32[4096]{0:T(1024)S(1)} %bitcast.241, bf16[1024,4096]{1,0:T(8,128)(2,1)} %all-gather.9.cloned.1.call-done, f32[512,1024]{1,0:T(8,128)S(1)} %get-tuple-element.69, f32[1024]{0:T(1024)S(1)} %get-tuple-element.57, f32[1024]{0:T(1024)S(1)} %get-tuple-element.58, ...), kind=kOutput, calls=%fused_computation.16 | convolution fusion | flops 4310171648 | bytes 23097344 | tf_op jit(solution)/shard_map/dot_general | solution.py:15
  215.8 45.2 %all-gather.11.cloned.1.call-done = bf16[4096,1024]{1,0:T(8,128)(2,1)} async-done(((bf16[512,1024]{1,0:T(8,128)(2,1)}), bf16[4096,1024]{1,0:T(8,128)(2,1)}) %all-gather.11.cloned.1.call-update) | async-done | bytes 8388624 | tf_op jit(solution)/shard_map/all_gather | solution.py:95
  261.0 8.5 %fusion.103 = (f32[512]{0:T(512)S(1)}, f32[512,1024]{1,0:T(8,128)S(1)}) fusion(f32[1024]{0:T(1024)S(1)} %get-tuple-element.56, bf16[512,4096]{1,0:T(8,128)(2,1)} %get-tuple-element.70, bf16[4096,1024]{1,0:T(8,128)(2,1)} %all-gather.11.cloned.1.call-done, f32[1024]{0:T(1024)S(1)} %get-tuple-element.57, f32[1024]{0:T(1024)S(1)} %get-tuple-element.58, ...), kind=kOutput, calls=%fused_computation.175 | convolution fusion | flops 4298636800 | bytes 16795648 | tf_op jit(solution)/shard_map/dot_general | solution.py:15
  273.0 11.9 %convert_reduce_fusion = (f32[4096]{0:T(1024)S(1)}, bf16[512,4096]{1,0:T(8,128)(2,1)S(1)}) fusion(f32[512,4096]{1,0:T(8,128)} %get-tuple-element.71, f32[4096]{0:T(1024)S(1)} %bitcast.242, bf16[4096,1024]{1,0:T(8,128)(2,1)} %all-gather.11.cloned.1.call-done, f32[512,1024]{1,0:T(8,128)S(1)} %get-tuple-element.30), kind=kOutput, calls=%fused_computation.12 | convolution fusion | flops 4322750464 | bytes 23101440 | tf_op jit(solution)/shard_map/dot_general | solution.py:23
  285.0 5.2 multiply_reduce_fusion.2
  299.0 5.8 fusion.55
  304.8 13.5 %fusion.44 = bf16[2,256,16,64]{1,3,2,0:T(8,128)(2,1)} fusion(f32[2,16,256,256]{2,3,1,0:T(8,128)} %fusion.55, bf16[2,256,16,64]{1,0,3,2:T(2,128)(2,1)} %reshape.331, f32[2,16,256,256]{2,3,1,0:T(8,128)} %copy-done.41, f32[2,16,256]{2,1,0:T(8,128)S(1)} %get-tuple-element.66), kind=kOutput, calls=%fused_computation.72 | convolution fusion | flops 283648256 | bytes 18907136 | tf_op jit(solution)/shard_map/bhqk,bhqd->bhkd/dot_general | solution.py:189
  318.3 13.3 %convert_reduce_fusion.2 = (f32[16,64]{1,0:T(8,128)S(1)}, bf16[2,256,16,64]{1,3,2,0:T(8,128)(2,1)}) fusion(f32[2,16,256,256]{2,3,1,0:T(8,128)} %fusion.55, f32[2,16,256,256]{2,3,1,0:T(8,128)} %copy-done.41, f32[2,16,256]{2,1,0:T(8,128)S(1)} %get-tuple-element.66, bf16[2,256,16,64]{1,0,3,2:T(2,128)(2,1)S(1)} %copy-done.11), kind=kOutput, calls=%fused_computation.33 | convolution fusion | flops 284695808 | bytes 18911232 | tf_op jit(solution)/shard_map/bhqk,bhkd->bhqd/dot_general | solution.py:186
  331.6 5.2 convert_reduce_fusion.1
  350.1 9.8 %convolution_convert_fusion.1 = bf16[1024,4096]{1,0:T(8,128)(2,1)} fusion(bf16[512,4096]{1,0:T(8,128)(2,1)} %copy-done.42, f32[512,1024]{1,0:T(8,128)S(1)} %get-tuple-element.69, f32[1024]{0:T(1024)S(1)} %get-tuple-element.57, f32[1024]{0:T(1024)S(1)} %get-tuple-element.58, f32[512]{0:T(512)S(1)} %add_rsqrt_fusion.1, f32[512]{0:T(512)S(1)} %broadcast_multiply_fusion.4), kind=kOutput, calls=%fused_computation.21 | convolution fusion | flops 4301783040 | bytes 14692352 | tf_op jit(solution)/shard_map/dot_general | solution.py:19
  362.0 9.9 %convolution_convert_fusion = bf16[4096,1024]{1,0:T(8,128)(2,1)} fusion(bf16[512,4096]{1,0:T(8,128)(2,1)} %get-tuple-element.70, f32[512,1024]{1,0:T(8,128)S(1)} %copy-done.17), kind=kOutput, calls=%fused_computation.20 | convolution fusion | flops 4299685888 | bytes 14680064 | tf_op jit(solution)/shard_map/dot_general | solution.py:19
  377.3 44.2 %reduce-scatter.4.cloned.1.call-done = bf16[512,1024]{1,0:T(8,128)(2,1)} async-done(((bf16[4096,1024]{1,0:T(8,128)(2,1)}), bf16[512,1024]{1,0:T(8,128)(2,1)}) %reduce-scatter.4.cloned.1.call-update) | async-done | bytes 1048592 | tf_op jit(solution)/shard_map/reduce_scatter | solution.py:165
  421.6 75.0 %reduce-scatter.6.cloned.1.call-done = bf16[128,4096]{1,0:T(8,128)(2,1)} async-done(((bf16[1024,4096]{1,0:T(8,128)(2,1)}), bf16[128,4096]{1,0:T(8,128)(2,1)}) %reduce-scatter.6.cloned.1.call-update) | async-done | bytes 1048592 | tf_op jit(solution)/shard_map/reduce_scatter | solution.py:165
  496.6 74.7 %reduce-scatter.8.cloned.1.call-done = bf16[512,1024]{1,0:T(8,128)(2,1)} async-done(((bf16[4096,1024]{1,0:T(8,128)(2,1)}), bf16[512,1024]{1,0:T(8,128)(2,1)}) %reduce-scatter.8.cloned.1.call-update) | async-done | bytes 1048592 | tf_op jit(solution)/shard_map/reduce_scatter | solution.py:165
  571.4 43.1 %psum.29 = f32[8,1536]{1,0:T(8,128)S(1)} all-reduce(f32[8,1536]{1,0:T(8,128)S(1)} %constant_dynamic-update-slice_fusion), channel_id=1, replica_groups=mesh['shard'=8,'rep'=4] {'shard','rep'}, use_global_device_ids=true, to_apply=%region_23.25 | all-reduce | flops 12288 | bytes 98304 | tf_op jit(solution)/shard_map/psum | solution.py:227
  623.2 31.6 %all-gather.13.cloned.1.call-done = bf16[8,256,1024]{2,1,0:T(8,128)(2,1)} async-done(((bf16[2,256,1024]{2,1,0:T(8,128)(2,1)}), bf16[8,256,1024]{2,1,0:T(8,128)(2,1)}) %all-gather.13.cloned.1.call-update) | async-done | bytes 4194320 | tf_op jit(solution)/shard_map/all_gather | solution.py:156
  657.2 120.7 %all-reduce.3.cloned.1.call-done = (bf16[512,1024]{1,0:T(8,128)(2,1)}, bf16[128,4096]{1,0:T(8,128)(2,1)}, bf16[512,1024]{1,0:T(8,128)(2,1)}) async-done(((bf16[512,1024]{1,0:T(8,128)(2,1)}, bf16[128,4096]{1,0:T(8,128)(2,1)}, bf16[512,1024]{1,0:T(8,128)(2,1)}), (bf16[512,1024]{1,0:T(8,128)(2,1)}, bf16[128,4096]{1,0:T(8,128)(2,1)}, bf16[512,1024]{1,0:T(8,128)(2,1)})) %all-reduce.3.cloned.1.call-update) | async-done | bytes 3145744 | tf_op jit(solution)/shard_map/psum | solution.py:168
  (199 shorter events, 77.1 us)
Async XLA Ops:
  7.2 21.6 %copy-start = (s32[64]{0:T(128)S(1)}, s32[64]{0:T(128)}, u32[]{:S(2)}) copy-start(s32[64]{0:T(128)} %param.22) | copy-start | bytes 772
  7.2 86.0 %all-gather.15.cloned.1.call-start = ((), (), s32[]{:S(2)}) async-start(), calls=%async_computation.7 | async-start | bytes 5242880 | tf_op jit(solution)/shard_map/all_gather | solution.py:123
  7.9 140.6 %all-gather.7.cloned.1.call-start = ((), (), s32[]{:S(2)}) async-start(), calls=%async_computation.3 | async-start | bytes 9437184 | tf_op jit(solution)/shard_map/all_gather | solution.py:95
  10.2 6.8 copy-start.36
  10.2 7.0 copy-start.37
  10.3 7.2 copy-start.38
  10.3 7.4 copy-start.39
  10.3 7.6 copy-start.40
  10.3 7.8 copy-start.32
  10.3 194.5 %all-gather.9.cloned.1.call-start = ((), (), s32[]{:S(2)}) async-start(), calls=%async_computation.4 | async-start | bytes 9437184 | tf_op jit(solution)/shard_map/all_gather | solution.py:95
  11.1 249.9 %all-gather.11.cloned.1.call-start = ((), (), s32[]{:S(2)}) async-start(), calls=%async_computation.5 | async-start | bytes 9437184 | tf_op jit(solution)/shard_map/all_gather | solution.py:95
  11.6 409.9 %reduce-scatter.4.cloned.1.call-start = ((), (), s32[]{:S(2)}) async-start(), calls=%async_computation.8 | async-start | bytes 9437184 | tf_op jit(solution)/shard_map/reduce_scatter | solution.py:165
  148.5 7.3 copy-start.27
  157.4 18.8 %copy-start.12 = (bf16[2,256,16,64]{1,0,3,2:T(2,128)(2,1)}, bf16[2,256,16,64]{1,0,3,2:T(2,128)(2,1)S(1)}, u32[]{:S(2)}) copy-start(bf16[2,256,16,64]{1,0,3,2:T(2,128)(2,1)S(1)} %reshape.333) | copy-start | bytes 3145732
  270.7 14.2 %slice-start = ((s8[8388608]{0:T(1024)(128)(4,1)}), s8[4194304]{0:T(1024)(128)(4,1)S(1)}, s32[]{:S(2)}) async-start(s8[8388608]{0:T(1024)(128)(4,1)} %bitcast.245), calls=%async_computation.12 | async-start | bytes 8388608
  273.0 12.0 %copy-start.16 = (f32[512,1024]{1,0:T(8,128)}, f32[512,1024]{1,0:T(8,128)S(1)}, u32[]{:S(2)}) copy-start(f32[512,1024]{1,0:T(8,128)S(1)} %get-tuple-element.30) | copy-start | bytes 6291460
  273.0 12.0 %slice-start.1 = ((s8[8388608]{0:T(1024)(128)(4,1)}), s8[4194304]{0:T(1024)(128)(4,1)S(1)}, s32[]{:S(2)}) async-start(s8[8388608]{0:T(1024)(128)(4,1)} %bitcast.245), calls=%async_computation.13 | async-start | bytes 8388608
  304.8 13.5 %copy-start.11 = (bf16[2,256,16,64]{1,0,3,2:T(2,128)(2,1)S(1)}, bf16[2,256,16,64]{1,0,3,2:T(2,128)(2,1)}, u32[]{:S(2)}) copy-start(bf16[2,256,16,64]{1,0,3,2:T(2,128)(2,1)} %copy-done.10) | copy-start | bytes 3145732
  350.1 146.5 %reduce-scatter.6.cloned.1.call-start = ((), (), s32[]{:S(2)}) async-start(), calls=%async_computation.9 | async-start | bytes 9437184 | tf_op jit(solution)/shard_map/reduce_scatter | solution.py:165
  360.0 211.4 %reduce-scatter.8.cloned.1.call-start = ((), (), s32[]{:S(2)}) async-start(), calls=%async_computation.10 | async-start | bytes 9437184 | tf_op jit(solution)/shard_map/reduce_scatter | solution.py:165
  371.9 282.9 %all-gather.13.cloned.1.call-start = ((), (), s32[]{:S(2)}) async-start(), calls=%async_computation.6 | async-start | bytes 5242880 | tf_op jit(solution)/shard_map/all_gather | solution.py:156
  371.9 199.5 %copy-start.30 = (f32[1024]{0:T(1024)S(1)}, f32[1024]{0:T(1024)}, u32[]{:S(2)}) copy-start(f32[1024]{0:T(1024)} %get-tuple-element.24) | copy-start | bytes 12292
  371.9 243.9 %copy-start.19 = (bf16[8,1,128,1024]{3,2,1,0:T(8,128)(2,1)S(1)}, bf16[8,1,128,1024]{3,2,1,0:T(8,128)(2,1)}, u32[]{:S(2)}) copy-start(bf16[8,1,128,1024]{3,2,1,0:T(8,128)(2,1)} %get-tuple-element.35) | copy-start | bytes 6291460
  372.6 405.2 %all-reduce.3.cloned.1.call-start = ((), (), s32[]{:S(2)}) async-start(), calls=%async_computation.11 | async-start | bytes 6291456 | tf_op jit(solution)/shard_map/psum | solution.py:168
  (30 other events, 94.1 us)
Sparse Core Ops, SparseCore 0:
  9.6 83.5 all-gather.14
  95.6 52.8 all-gather.6
  150.4 54.3 all-gather.8
  206.6 54.3 all-gather.10
  350.2 71.2 reduce-scatter.3
  425.3 71.2 reduce-scatter.5
  500.0 71.2 reduce-scatter.7
  573.0 81.7 all-gather.12
  657.6 120.2 all-reduce.2
where the time goes:
time: 794 us; the launch traced here: 790 us
  waiting for transfers between devices  530 us (67%)
  matrix products  123 us (15%)
  blocking collectives  53.8 us (7%)
  local copies, waits for them, and re-layouts  40.2 us (5%)
  between operations  22.6 us (3%)
  other arithmetic  20 us (3%)
    reduce_scatter x3, waiting for transfers between devices, reduced(): return lax.psum_scatter(part, 'shard', scatter_dimension=0, tiled=True)  194 us
    psum x1, waiting for transfers between devices, over_rep(): return lax.psum(part, 'rep').astype(F32)  121 us
    all_gather x3, waiting for transfers between devices, gather(): return lax.all_gather(block, 'shard', axis=0, tiled=True)  119 us
    all_gather x1, waiting for transfers between devices, local(): cot = pick(lax.all_gather(cotangent, 'rep', axis=0, tiled=True), wanted)  62.3 us
    psum x1, blocking collectives, local(): g_vec = lax.psum(g_vec, ('shard', 'rep'))  43.1 us
    all_gather x1, waiting for transfers between devices, local(): layer_out = pick(lax.all_gather(out, 'rep', axis=0, tiled=True), sources)  31.6 us
    dot_general x6, matrix products, matmul(): return jnp.dot(left, right, preferred_element_type=F32)  31.3 us
    dot_general x6, matrix products, right_trans(): lax.dot_general(left, right, (((1,), (1,)), ((), ())), preferred_element_...  25.8 us
  transfers between devices with their start and end apart: 9, of which 9 were waited for; matrix products, arithmetic and copies ran while one was open for 10% of the time, Pallas kernels for 0%

commit v1 on v0

--- a/solution.py
+++ b/solution.py
@@ -165,7 +165,7 @@
         return lax.psum_scatter(part, "shard", scatter_dimension=0, tiled=True)
 
     def over_rep(part):
-        return lax.psum(part, "rep").astype(F32)
+        return jnp.sum(lax.all_gather(part, "rep"), axis=0).astype(F32)
 
     g_down = reduced(left_trans(act_low, grad_sum_low).astype(BF16))
     grad_pre = (right_trans(grad_sum_low, full_down) * slope).astype(BF16)

time: 794 us -> 913 us (1.15)
  waiting for transfers between devices: 530 us -> 640 us
  other arithmetic: 20 us -> 29.7 us
    all_gather x0 -> x3, waiting for transfers between devices: none -> 231 us  [over_rep(): return jnp.sum(lax.all_gather(part, 'rep'), axis=0).astype(F32)]
    psum x1 -> x0, waiting for transfers between devices: 121 us -> none  [over_rep(): return lax.psum(part, 'rep').astype(F32)]
    reduce_sum x0 -> x3, other arithmetic: none -> 9.72 us  [over_rep(): return jnp.sum(lax.all_gather(part, 'rep'), axis=0).astype(F32)]
  transfers between devices with their start and end apart: 9 -> 11, of which waited for: 9 -> 11; matrix products, arithmetic and copies ran while one was open for 10% -> 10% of each run, Pallas kernels for 0% -> 0%
where the time goes in v1:
time: 913 us; the launch traced here: 909 us
  waiting for transfers between devices  640 us (70%)
  matrix products  123 us (13%)
  blocking collectives  54.2 us (6%)
  local copies, waits for them, and re-layouts  38.8 us (4%)
  other arithmetic  29.7 us (3%)
  between operations  22.6 us (2%)
    all_gather x3, waiting for transfers between devices, over_rep(): return jnp.sum(lax.all_gather(part, 'rep'), axis=0).astype(F32)  231 us
    reduce_scatter x3, waiting for transfers between devices, reduced(): return lax.psum_scatter(part, 'shard', scatter_dimension=0, tiled=True)  198 us
    all_gather x3, waiting for transfers between devices, gather(): return lax.all_gather(block, 'shard', axis=0, tiled=True)  119 us
    all_gather x1, waiting for transfers between devices, local(): cot = pick(lax.all_gather(cotangent, 'rep', axis=0, tiled=True), wanted)  62.3 us
    psum x1, blocking collectives, local(): g_vec = lax.psum(g_vec, ('shard', 'rep'))  43.6 us
    dot_general x6, matrix products, matmul(): return jnp.dot(left, right, preferred_element_type=F32)  31.3 us
    all_gather x1, waiting for transfers between devices, local(): layer_out = pick(lax.all_gather(out, 'rep', axis=0, tiled=True), sources)  26.5 us
    dot_general x6, matrix products, right_trans(): lax.dot_general(left, right, (((1,), (1,)), ((), ())), preferred_element_...  25.8 us
  transfers between devices with their start and end apart: 11, of which 11 were waited for; matrix products, arithmetic and copies ran while one was open for 10% of the time, Pallas kernels for 0%

profile of v1, /device:TPU:0, one launch (start us, length us, event | category | flops | bytes accessed | tf_op | source)
XLA Modules:
  0.0 909.0 jit_solution(15696778140888207360)
XLA Ops:
  18.1 10.6 %all-gather.3 = bf16[8,1,1536]{2,1,0:T(2,128)(2,1)S(1)} all-gather(bf16[1,1,1536]{2,1,0:T(2,128)(2,1)S(1)} %reshape.386), channel_id=1, replica_groups=mesh['shard'=8,'rep'=4] {'shard'}, dimensions={0}, use_global_device_ids=true | all-gather | bytes 27648 | tf_op jit(solution)/shard_map/all_gather | solution.py:102
  30.9 62.3 %all-gather.21.cloned.1.call-done = bf16[8,256,1024]{2,1,0:T(8,128)(2,1)} async-done(((bf16[2,256,1024]{2,1,0:T(8,128)(2,1)}), bf16[8,256,1024]{2,1,0:T(8,128)(2,1)}) %all-gather.21.cloned.1.call-update) | async-done | bytes 4194320 | tf_op jit(solution)/shard_map/all_gather | solution.py:123
  95.5 53.0 %all-gather.13.cloned.1.call-done = bf16[4096,1024]{1,0:T(8,128)(2,1)} async-done(((bf16[512,1024]{1,0:T(8,128)(2,1)}), bf16[4096,1024]{1,0:T(8,128)(2,1)}) %all-gather.13.cloned.1.call-update) | async-done | bytes 8388624 | tf_op jit(solution)/shard_map/all_gather | solution.py:95
  148.5 5.9 fusion.97
  183.9 21.0 %all-gather.15.cloned.1.call-done = bf16[1024,4096]{1,0:T(8,128)(2,1)} async-done(((bf16[128,4096]{1,0:T(8,128)(2,1)}), bf16[1024,4096]{1,0:T(8,128)(2,1)}) %all-gather.15.cloned.1.call-update) | async-done | bytes 8388624 | tf_op jit(solution)/shard_map/all_gather | solution.py:95
  204.8 10.9 %multiply_convert_fusion.1 = (bf16[512,4096]{1,0:T(8,128)(2,1)}, f32[512,4096]{1,0:T(8,128)}) fusion(f32[4096]{0:T(1024)S(1)} %bitcast.247, bf16[1024,4096]{1,0:T(8,128)(2,1)} %all-gather.15.cloned.1.call-done, f32[512,1024]{1,0:T(8,128)S(1)} %get-tuple-element.66, f32[1024]{0:T(1024)S(1)} %get-tuple-element.54, f32[1024]{0:T(1024)S(1)} %get-tuple-element.55, ...), kind=kOutput, calls=%fused_computation.16 | convolution fusion | flops 4310171648 | bytes 23097344 | tf_op jit(solution)/shard_map/dot_general | solution.py:15
  215.8 45.2 %all-gather.17.cloned.1.call-done = bf16[4096,1024]{1,0:T(8,128)(2,1)} async-done(((bf16[512,1024]{1,0:T(8,128)(2,1)}), bf16[4096,1024]{1,0:T(8,128)(2,1)}) %all-gather.17.cloned.1.call-update) | async-done | bytes 8388624 | tf_op jit(solution)/shard_map/all_gather | solution.py:95
  261.0 8.5 fusion.103
  273.0 12.0 %convert_reduce_fusion = (f32[4096]{0:T(1024)S(1)}, bf16[512,4096]{1,0:T(8,128)(2,1)S(1)}) fusion(f32[512,4096]{1,0:T(8,128)} %get-tuple-element.68, f32[4096]{0:T(1024)S(1)} %bitcast.248, bf16[4096,1024]{1,0:T(8,128)(2,1)} %all-gather.17.cloned.1.call-done, f32[512,1024]{1,0:T(8,128)S(1)} %get-tuple-element.27), kind=kOutput, calls=%fused_computation.12 | convolution fusion | flops 4322750464 | bytes 23101440 | tf_op jit(solution)/shard_map/dot_general | solution.py:23
  285.0 5.2 multiply_reduce_fusion.2
  299.0 5.7 fusion.55
  304.7 13.5 %fusion.44 = bf16[2,256,16,64]{1,3,2,0:T(8,128)(2,1)} fusion(f32[2,16,256,256]{2,3,1,0:T(8,128)} %fusion.55, bf16[2,256,16,64]{1,0,3,2:T(2,128)(2,1)} %reshape.331, f32[2,16,256,256]{2,3,1,0:T(8,128)} %copy-done.39, f32[2,16,256]{2,1,0:T(8,128)S(1)} %get-tuple-element.63), kind=kOutput, calls=%fused_computation.72 | convolution fusion | flops 283648256 | bytes 18907136 | tf_op jit(solution)/shard_map/bhqk,bhqd->bhkd/dot_general | solution.py:189
  318.2 13.3 %convert_reduce_fusion.2 = (f32[16,64]{1,0:T(8,128)S(1)}, bf16[2,256,16,64]{1,3,2,0:T(8,128)(2,1)}) fusion(f32[2,16,256,256]{2,3,1,0:T(8,128)} %fusion.55, f32[2,16,256,256]{2,3,1,0:T(8,128)} %copy-done.39, f32[2,16,256]{2,1,0:T(8,128)S(1)} %get-tuple-element.63, bf16[2,256,16,64]{1,0,3,2:T(2,128)(2,1)S(1)} %copy-done.11), kind=kOutput, calls=%fused_computation.33 | convolution fusion | flops 284695808 | bytes 18911232 | tf_op jit(solution)/shard_map/bhqk,bhkd->bhqd/dot_general | solution.py:186
  331.5 5.2 convert_reduce_fusion.1
  350.1 9.8 %convolution_convert_fusion.1 = bf16[1024,4096]{1,0:T(8,128)(2,1)} fusion(bf16[512,4096]{1,0:T(8,128)(2,1)} %copy-done.40, f32[512,1024]{1,0:T(8,128)S(1)} %get-tuple-element.66, f32[1024]{0:T(1024)S(1)} %get-tuple-element.54, f32[1024]{0:T(1024)S(1)} %get-tuple-element.55, f32[512]{0:T(512)S(1)} %add_rsqrt_fusion.1, f32[512]{0:T(512)S(1)} %broadcast_multiply_fusion.4), kind=kOutput, calls=%fused_computation.21 | convolution fusion | flops 4301783040 | bytes 14692352 | tf_op jit(solution)/shard_map/dot_general | solution.py:19
  361.9 9.9 %convolution_convert_fusion = bf16[4096,1024]{1,0:T(8,128)(2,1)} fusion(bf16[512,4096]{1,0:T(8,128)(2,1)} %get-tuple-element.67, f32[512,1024]{1,0:T(8,128)S(1)} %copy-done.17), kind=kOutput, calls=%fused_computation.20 | convolution fusion | flops 4299685888 | bytes 14680064 | tf_op jit(solution)/shard_map/dot_general | solution.py:19
  372.6 48.8 %reduce-scatter.4.cloned.1.call-done = bf16[512,1024]{1,0:T(8,128)(2,1)} async-done(((bf16[4096,1024]{1,0:T(8,128)(2,1)}), bf16[512,1024]{1,0:T(8,128)(2,1)}) %reduce-scatter.4.cloned.1.call-update) | async-done | bytes 1048592 | tf_op jit(solution)/shard_map/reduce_scatter | solution.py:165
  421.5 74.9 %reduce-scatter.6.cloned.1.call-done = bf16[128,4096]{1,0:T(8,128)(2,1)} async-done(((bf16[1024,4096]{1,0:T(8,128)(2,1)}), bf16[128,4096]{1,0:T(8,128)(2,1)}) %reduce-scatter.6.cloned.1.call-update) | async-done | bytes 1048592 | tf_op jit(solution)/shard_map/reduce_scatter | solution.py:165
  496.5 74.7 %reduce-scatter.8.cloned.1.call-done = bf16[512,1024]{1,0:T(8,128)(2,1)} async-done(((bf16[4096,1024]{1,0:T(8,128)(2,1)}), bf16[512,1024]{1,0:T(8,128)(2,1)}) %reduce-scatter.8.cloned.1.call-update) | async-done | bytes 1048592 | tf_op jit(solution)/shard_map/reduce_scatter | solution.py:165
  575.9 43.6 %psum.7 = f32[8,1536]{1,0:T(8,128)S(1)} all-reduce(f32[8,1536]{1,0:T(8,128)S(1)} %constant_dynamic-update-slice_fusion), channel_id=1, replica_groups=mesh['shard'=8,'rep'=4] {'shard','rep'}, use_global_device_ids=true, to_apply=%region_23.25 | all-reduce | flops 12288 | bytes 98304 | tf_op jit(solution)/shard_map/psum | solution.py:227
  628.1 26.5 %all-gather.19.cloned.1.call-done = bf16[8,256,1024]{2,1,0:T(8,128)(2,1)} async-done(((bf16[2,256,1024]{2,1,0:T(8,128)(2,1)}), bf16[8,256,1024]{2,1,0:T(8,128)(2,1)}) %all-gather.19.cloned.1.call-update) | async-done | bytes 4194320 | tf_op jit(solution)/shard_map/all_gather | solution.py:156
  656.9 78.6 %all-gather.23.cloned.1.call-done = bf16[2048,1024]{1,0:T(8,128)(2,1)} async-done(((bf16[512,1024]{1,0:T(8,128)(2,1)}), bf16[2048,1024]{1,0:T(8,128)(2,1)}) %all-gather.23.cloned.1.call-update) | async-done | bytes 4194320 | tf_op jit(solution)/shard_map/all_gather | solution.py:168
  738.9 77.5 %all-gather.25.cloned.1.call-done = bf16[512,4096]{1,0:T(8,128)(2,1)} async-done(((bf16[128,4096]{1,0:T(8,128)(2,1)}), bf16[512,4096]{1,0:T(8,128)(2,1)}) %all-gather.25.cloned.1.call-update) | async-done | bytes 4194320 | tf_op jit(solution)/shard_map/all_gather | solution.py:168
  822.4 75.0 %all-gather.27.cloned.1.call-done = bf16[2048,1024]{1,0:T(8,128)(2,1)} async-done(((bf16[512,1024]{1,0:T(8,128)(2,1)}), bf16[2048,1024]{1,0:T(8,128)(2,1)}) %all-gather.27.cloned.1.call-update) | async-done | bytes 4194320 | tf_op jit(solution)/shard_map/all_gather | solution.py:168
  (204 shorter events, 94.7 us)
Async XLA Ops:
  7.2 21.6 %copy-start = (s32[64]{0:T(128)S(1)}, s32[64]{0:T(128)}, u32[]{:S(2)}) copy-start(s32[64]{0:T(128)} %param.22) | copy-start | bytes 772
  7.2 86.0 %all-gather.21.cloned.1.call-start = ((), (), s32[]{:S(2)}) async-start(), calls=%async_computation.7 | async-start | bytes 5242880 | tf_op jit(solution)/shard_map/all_gather | solution.py:123
  7.9 140.6 %all-gather.13.cloned.1.call-start = ((), (), s32[]{:S(2)}) async-start(), calls=%async_computation.3 | async-start | bytes 9437184 | tf_op jit(solution)/shard_map/all_gather | solution.py:95
  10.3 7.4 copy-start.37
  10.3 7.6 copy-start.38
  10.3 7.8 copy-start.30
  10.3 194.5 %all-gather.15.cloned.1.call-start = ((), (), s32[]{:S(2)}) async-start(), calls=%async_computation.4 | async-start | bytes 9437184 | tf_op jit(solution)/shard_map/all_gather | solution.py:95
  11.1 249.9 %all-gather.17.cloned.1.call-start = ((), (), s32[]{:S(2)}) async-start(), calls=%async_computation.5 | async-start | bytes 9437184 | tf_op jit(solution)/shard_map/all_gather | solution.py:95
  11.6 409.8 %reduce-scatter.4.cloned.1.call-start = ((), (), s32[]{:S(2)}) async-start(), calls=%async_computation.8 | async-start | bytes 9437184 | tf_op jit(solution)/shard_map/reduce_scatter | solution.py:165
  148.5 7.2 copy-start.25
  157.4 18.8 %copy-start.12 = (bf16[2,256,16,64]{1,0,3,2:T(2,128)(2,1)}, bf16[2,256,16,64]{1,0,3,2:T(2,128)(2,1)S(1)}, u32[]{:S(2)}) copy-start(bf16[2,256,16,64]{1,0,3,2:T(2,128)(2,1)S(1)} %reshape.333) | copy-start | bytes 3145732
  270.7 14.2 %slice-start = ((s8[8388608]{0:T(1024)(128)(4,1)}), s8[4194304]{0:T(1024)(128)(4,1)S(1)}, s32[]{:S(2)}) async-start(s8[8388608]{0:T(1024)(128)(4,1)} %bitcast.251), calls=%async_computation.14 | async-start | bytes 8388608
  273.0 12.0 %copy-start.16 = (f32[512,1024]{1,0:T(8,128)}, f32[512,1024]{1,0:T(8,128)S(1)}, u32[]{:S(2)}) copy-start(f32[512,1024]{1,0:T(8,128)S(1)} %get-tuple-element.27) | copy-start | bytes 6291460
  273.0 12.0 %slice-start.1 = ((s8[8388608]{0:T(1024)(128)(4,1)}), s8[4194304]{0:T(1024)(128)(4,1)S(1)}, s32[]{:S(2)}) async-start(s8[8388608]{0:T(1024)(128)(4,1)} %bitcast.251), calls=%async_computation.15 | async-start | bytes 8388608
  304.7 13.5 %copy-start.11 = (bf16[2,256,16,64]{1,0,3,2:T(2,128)(2,1)S(1)}, bf16[2,256,16,64]{1,0,3,2:T(2,128)(2,1)}, u32[]{:S(2)}) copy-start(bf16[2,256,16,64]{1,0,3,2:T(2,128)(2,1)} %copy-done.10) | copy-start | bytes 3145732
  350.0 146.4 %reduce-scatter.6.cloned.1.call-start = ((), (), s32[]{:S(2)}) async-start(), calls=%async_computation.9 | async-start | bytes 9437184 | tf_op jit(solution)/shard_map/reduce_scatter | solution.py:165
  359.9 211.3 %reduce-scatter.8.cloned.1.call-start = ((), (), s32[]{:S(2)}) async-start(), calls=%async_computation.10 | async-start | bytes 9437184 | tf_op jit(solution)/shard_map/reduce_scatter | solution.py:165
  371.8 282.8 %all-gather.19.cloned.1.call-start = ((), (), s32[]{:S(2)}) async-start(), calls=%async_computation.6 | async-start | bytes 5242880 | tf_op jit(solution)/shard_map/all_gather | solution.py:156
  371.8 199.3 %copy-start.29 = (s32[2]{0:T(128)S(1)}, s32[2]{0:T(128)}, u32[]{:S(2)}) copy-start(s32[2]{0:T(128)} %get-tuple-element.78) | copy-start | bytes 28
  371.9 204.0 %copy-start.28 = (f32[1024]{0:T(1024)S(1)}, f32[1024]{0:T(1024)}, u32[]{:S(2)}) copy-start(f32[1024]{0:T(1024)} %get-tuple-element.24) | copy-start | bytes 12292
  371.9 248.9 %copy-start.19 = (bf16[8,1,128,1024]{3,2,1,0:T(8,128)(2,1)S(1)}, bf16[8,1,128,1024]{3,2,1,0:T(8,128)(2,1)}, u32[]{:S(2)}) copy-start(bf16[8,1,128,1024]{3,2,1,0:T(8,128)(2,1)} %get-tuple-element.32) | copy-start | bytes 6291460
  372.5 363.0 %all-gather.23.cloned.1.call-start = ((), (), s32[]{:S(2)}) async-start(), calls=%async_computation.11 | async-start | bytes 5242880 | tf_op jit(solution)/shard_map/all_gather | solution.py:168
  421.4 394.9 %all-gather.25.cloned.1.call-start = ((), (), s32[]{:S(2)}) async-start(), calls=%async_computation.12 | async-start | bytes 5242880 | tf_op jit(solution)/shard_map/all_gather | solution.py:168
  496.4 400.9 %all-gather.27.cloned.1.call-start = ((), (), s32[]{:S(2)}) async-start(), calls=%async_computation.13 | async-start | bytes 5242880 | tf_op jit(solution)/shard_map/all_gather | solution.py:168
  (30 other events, 111.8 us)
Sparse Core Ops, SparseCore 0:
  9.6 83.5 all-gather.20
  95.6 52.8 all-gather.12
  150.4 54.3 all-gather.14
  206.6 54.3 all-gather.16
  350.1 71.2 reduce-scatter.3
  425.1 71.2 reduce-scatter.5
  499.9 71.2 reduce-scatter.7
  572.8 81.7 all-gather.18
  656.2 79.2 all-gather.22
  737.0 79.2 all-gather.24
  818.0 79.2 all-gather.26
